TPU v7x, 256 devices: a whole 4x4x8 slice. The times are simulated.
256 devices in a mesh: shell: 128 (over x, y, z), radial: 2 (over core).
Axes of the slice: x: 4, y: 4, z: 8, core: 2. Of those that a mesh axis runs over, the one named last changes fastest.
Arguments:
- state: float32 [8, 32, 1024, 128], P(None, 'radial', 'shell')
- footpoints: int32 [32, 1024, 128], P('radial', 'shell'), may hold values from 0 to 32767, as said below
- conductance: float32 [4, 128, 256], P(None, 'shell', 'radial'), may hold values from 0.1 to 0.45
- inverse_blocks: float32 [128, 2, 128, 128], P('shell', 'radial')
Outputs:
- state_next: float32 [8, 32, 1024, 128], P(None, 'radial', 'shell')
- potential: float32 [128, 256], P('shell', 'radial')
- footpoint_potential: float32 [32, 1024, 128], P('radial', 'shell')
Inputs may be any that keep to these rules, and one draw needn't show every extreme that they name: `footpoints`: A cell whose longitude index lon lies in shell block s = lon // 8 maps to a node whose column (node % 256) lies in s * 2 to (s + 1) * 2 - 1.
All inputs are finite; a program needn't handle non-finite values.
Results may differ from a plain program's by a relative error of at most 0.0003.
Values sent between devices are 32-bit elements; how exact they have to be, the bound alone decides.
A program may use at most 64 MiB of HBM per device.

v0:
```python
import jax
import jax.numpy as jnp
from jax import lax
from jax.sharding import PartitionSpec as P

NLAT_I = 128
NLON_I = 256
ITERS_I = 4
GAMMA = 5.0 / 3.0
TIME_STEP = 0.02
CELL_AREA = 0.125


def padded_2(block, sides, width, periodic):
    for axis, dim in sides:
        count = lax.axis_size(axis)
        forward = [(i, i + 1) for i in range(count - 1)]
        if periodic:
            forward.append((count - 1, 0))
        backward = [(target, source) for source, target in forward]
        low = lax.ppermute(
            lax.slice_in_dim(block, block.shape[dim] - width, None, axis=dim), axis, forward
        )
        high = lax.ppermute(lax.slice_in_dim(block, 0, width, axis=dim), axis, backward)
        block = jnp.concatenate([low, block, high], axis=dim)
    return block


def minmod(first_jump, second_jump):
    return (
        0.5
        * (jnp.sign(first_jump) + jnp.sign(second_jump))
        * jnp.minimum(jnp.abs(first_jump), jnp.abs(second_jump))
    )


def physical_flux(conserved, direction):
    density = conserved[0]
    velocity = conserved[1:4] / density
    magnetic = conserved[4:7]
    energy = conserved[7]
    field_sq = jnp.sum(magnetic * magnetic, axis=0)
    kinetic = jnp.sum(velocity * velocity, axis=0)
    pressure = (GAMMA - 1.0) * (energy - 0.5 * density * kinetic - 0.5 * field_sq)
    total_pressure = pressure + 0.5 * field_sq
    normal_speed = velocity[direction]
    normal_field = magnetic[direction]
    selector = (jnp.arange(3) == direction).astype(jnp.float32).reshape((3,) + (1,) * density.ndim)
    momentum_flux = (
        density * velocity * normal_speed - magnetic * normal_field + total_pressure * selector
    )
    induction = normal_speed * magnetic - normal_field * velocity
    alignment = jnp.sum(velocity * magnetic, axis=0)
    energy_flux = (energy + total_pressure) * normal_speed - normal_field * alignment
    fluxes = jnp.concatenate(
        [(density * normal_speed)[None], momentum_flux, induction, energy_flux[None]], axis=0
    )
    signal = jnp.abs(normal_speed) + jnp.sqrt((GAMMA * jnp.abs(pressure) + field_sq) / density)
    return (fluxes, signal)


def face_divergence(padded, direction):
    dimension = direction + 1
    cell_count = padded.shape[dimension] - 4

    def window_slice(array, first_index, length):
        return lax.slice_in_dim(array, first_index, first_index + length, axis=dimension)

    jumps = window_slice(padded, 1, cell_count + 3) - window_slice(padded, 0, cell_count + 3)
    slopes = minmod(window_slice(jumps, 1, cell_count + 2), window_slice(jumps, 0, cell_count + 2))
    left_state = window_slice(padded, 1, cell_count + 1) + 0.5 * window_slice(
        slopes, 0, cell_count + 1
    )
    right_state = window_slice(padded, 2, cell_count + 1) - 0.5 * window_slice(
        slopes, 1, cell_count + 1
    )
    left_flux, left_signal = physical_flux(left_state, direction)
    right_flux, right_signal = physical_flux(right_state, direction)
    signal_max = jnp.maximum(left_signal, right_signal)
    face_flux = 0.5 * (left_flux + right_flux) - 0.5 * signal_max * (right_state - left_state)
    return window_slice(face_flux, 1, cell_count) - window_slice(face_flux, 0, cell_count)


def tendency(padded):
    total_div = face_divergence(padded[:, :, 2:-2, 2:-2], 0)
    total_div = total_div + face_divergence(padded[:, 2:-2, :, 2:-2], 1)
    total_div = total_div + face_divergence(padded[:, 2:-2, 2:-2, :], 2)
    return -total_div


def shifted(values, direction, offset):
    for dimension in range(3):
        first_index = offset if dimension == direction else 2
        length = values.shape[dimension] - 4
        values = lax.slice_in_dim(values, first_index, first_index + length, axis=dimension)
    return values


def field_current(padded):
    magnetic = padded[4:7]

    def derivative(component, direction):
        return 0.5 * (
            shifted(magnetic[component], direction, 3) - shifted(magnetic[component], direction, 1)
        )

    curl_first = derivative(2, 1) - derivative(1, 2)
    curl_second = derivative(0, 2) - derivative(2, 0)
    curl_third = derivative(1, 0) - derivative(0, 1)
    centre = [shifted(magnetic[component], 0, 2) for component in range(3)]
    field_sq = centre[0] * centre[0] + centre[1] * centre[1] + centre[2] * centre[2]
    aligned = curl_first * centre[0] + curl_second * centre[1] + curl_third * centre[2]
    return CELL_AREA * aligned / jnp.sqrt(1.0 + field_sq)


def pad_latitude(field):
    return jnp.pad(field, ((0, 0), (0, 0), (0, 0), (2, 2)), mode="edge")


def fill_radial(field, margin):
    position = lax.axis_index("radial")
    last_index = lax.axis_size("radial") - 1
    extent = field.shape[1]
    layer_index = lax.broadcasted_iota(jnp.int32, (1, extent, 1, 1), 1)
    lower_edge = lax.slice_in_dim(field, margin, margin + 1, axis=1)
    upper_edge = lax.slice_in_dim(field, extent - margin - 1, extent - margin, axis=1)
    field = jnp.where((layer_index < margin) & (position == 0), lower_edge, field)
    return jnp.where((layer_index >= extent - margin) & (position == last_index), upper_edge, field)


def extended_cells(field):
    grown = padded_2(field, (("shell", 2), ("radial", 1)), 2, True)
    return pad_latitude(fill_radial(grown, 2))


def body(state, footpoints, conductance, inverse_blocks):
    first_padded = extended_cells(state)
    section_one = state + TIME_STEP * tendency(first_padded)
    second_padded = extended_cells(section_one)
    state_next = 0.5 * state + 0.5 * (section_one + TIME_STEP * tendency(second_padded))
    cell_current = field_current(first_padded).reshape(-1)
    rows_owned = inverse_blocks.shape[0]
    half_width = inverse_blocks.shape[2]
    halves_count = lax.axis_size("radial")
    latitude_node = footpoints // NLON_I
    column_node = footpoints % NLON_I
    owner_index = latitude_node // rows_owned * halves_count + column_node // half_width
    node_slot = (
        owner_index * (rows_owned * half_width)
        + latitude_node % rows_owned * half_width
        + column_node % half_width
    )
    partial_sums = jax.ops.segment_sum(
        cell_current, node_slot.reshape(-1), num_segments=NLAT_I * NLON_I
    )
    currents = lax.psum_scatter(
        partial_sums, ("shell", "radial"), scatter_dimension=0, tiled=True
    ).reshape(rows_owned, half_width)
    block_matrices = inverse_blocks[:, 0]

    def apply_blocks(vector):
        return jnp.einsum("rij,rj->ri", block_matrices, vector, precision=lax.Precision.HIGHEST)

    potential = apply_blocks(currents)
    for sweep_index in range(ITERS_I - 1):
        padded_panel = padded_2(potential, (("shell", 0), ("radial", 1)), 1, False)
        coupled = currents + conductance[0] * padded_panel[:-2, 1:-1]
        coupled = coupled + conductance[1] * padded_panel[2:, 1:-1]
        coupled = coupled + conductance[2] * padded_panel[1:-1, :-2]
        coupled = coupled + conductance[3] * padded_panel[1:-1, 2:]
        potential = apply_blocks(coupled)
    whole_table = lax.all_gather(potential.reshape(-1), ("shell", "radial"), axis=0, tiled=True)
    footpoint_potential = whole_table[node_slot]
    return (state_next, potential, footpoint_potential)


def solution(mesh):
    return jax.shard_map(
        body,
        mesh=mesh,
        in_specs=(
            P(None, "radial", "shell", None),
            P("radial", "shell", None),
            P(None, "shell", "radial"),
            P("shell", "radial", None, None),
        ),
        out_specs=(
            P(None, "radial", "shell", None),
            P("shell", "radial"),
            P("radial", "shell", None),
        ),
        check_vma=False,
    )
```

profile of v0, /device:TPU:1, one launch (start us, length us, event | category | flops | bytes accessed | tf_op | source)
XLA Modules:
  0.0 684.3 jit_solution(17312191880690666836)
XLA Ops:
  7.2 1.4 fusion.271
  8.6 2.5 collective-permute-start
  11.1 8.7 %collective-permute-start.1 = (f32[8,16,2,128]{3,2,1,0:T(2,128)S(1)}, f32[8,16,2,128]{3,2,1,0:T(2,128)S(1)}, u32[]{:S(2)}, u32[]{:S(2)}) collective-permute-start(f32[8,16,2,128]{3,2,1,0:T(2,128)S(1)} %get-tuple-element.179), channel_id=1, source_target_pairs={{2,0},{4,2},{6,4},{8,6},{10,8},{12,10},{14,12},{16,14},{18,16},{20... | collective-permute-start | bytes 393224 | tf_op jit(solution)/shard_map/ppermute | solution.py:24
  20.9 1.6 fusion.158
  23.2 0.9 pad_maximum_fusion.19
  24.1 1.1 collective-permute-start.2
  26.9 0.9 slice_subtract_fusion.4
  27.8 1.1 slice_subtract_fusion.2
  28.9 1.6 fusion.269
  30.5 2.5 copy.843
  33.0 1.2 copy.844
  36.1 2.6 pad_maximum_fusion
  39.9 1.5 multiply_reduce_fusion.31
  42.6 1.8 multiply_reduce_fusion.22
  45.0 1.6 multiply_reduce_fusion.19
  49.1 86.9 %scatter_custom_fusion = f32[32768]{0:T(1024)} fusion(s32[16384]{0:T(1024)} %bitcast.618, f32[16384]{0:T(1024)} %bitcast.619, f32[]{:T(128)} %constant.97.clone.1), kind=kCustom, calls=%fused_computation.431 | custom fusion | flops 16384 | bytes 131584 | tf_op jit(solution)/shard_map/scatter-add | solution.py:153
  136.0 2.6 slice_subtract_fusion.1
  147.7 1.3 fusion.14
  149.0 0.9 multiply_add_fusion.10
  149.9 228.3 %all-reduce.3.cloned.1.call-done = f32[32768]{0:T(1024)} async-done(((f32[32768]{0:T(1024)}), f32[32768]{0:T(1024)}) %all-reduce.3.cloned.1.call-update) | async-done | bytes 131088
  379.1 1.3 collective-permute-start.9
  380.5 4.4 collective-permute-start.8
  384.9 1.4 fusion.24
  386.4 1.3 collective-permute-start.10
  387.7 4.2 collective-permute-start.11
  392.9 1.5 collective-permute-start.13
  394.3 4.3 collective-permute-start.12
  399.5 1.3 collective-permute-start.14
  400.8 3.1 collective-permute-start.15
  404.9 1.3 collective-permute-start.17
  406.2 4.5 collective-permute-start.16
  410.9 1.8 collective-permute-start.4
  412.7 5.2 collective-permute-start.5
  417.9 1.3 collective-permute-start.18
  419.2 3.1 collective-permute-start.19
  423.4 61.8 %all-gather = f32[256,1,128]{2,1,0:T(1,128)S(1)} all-gather(f32[1,1,128]{2,1,0:T(1,128)S(1)} %bitcast.621), channel_id=1, replica_groups=mesh['shell'=128,'radial'=2] {'shell','radial'}, dimensions={0}, use_global_device_ids=true | all-gather | bytes 131584 | tf_op jit(solution)/shard_map/all_gather | solution.py:172
  485.1 160.6 %gather_fusion = f32[16384]{0:T(1024)} fusion(f32[32768]{0:T(1024)S(1)} %bitcast.598, s32[16384]{0:T(1024)S(1)} %copy-done.67), kind=kCustom, calls=%fused_computation | custom fusion | bytes 196608 | tf_op jit(solution)/shard_map/gather | solution.py:173
  646.4 0.8 collective-permute-done.6
  648.2 1.9 fusion.268
  650.5 1.4 multiply_reduce_fusion.28
  652.0 1.4 multiply_reduce_fusion.25
  654.6 1.8 multiply_reduce_fusion.10
  657.0 1.6 multiply_reduce_fusion.7
  659.3 3.2 copy.860
  662.5 3.2 copy.861
  665.7 1.3 reshape.264
  667.4 1.0 fusion.4
  676.4 1.1 fusion.32
  (276 shorter events, 37.0 us)
Async XLA Ops:
  7.2 371.8 %copy-start = (f32[1,1,128,128]{3,2,1,0:T(8,128)S(1)}, f32[1,1,128,128]{3,2,1,0:T(8,128)}, u32[]{:S(2)}) copy-start(f32[1,1,128,128]{3,2,1,0:T(8,128)} %param.7) | copy-start | bytes 196612
  7.2 18.3 %copy-start.4 = (f32[8,16,8,128]{3,2,1,0:T(8,128)S(1)}, f32[8,16,8,128]{3,2,1,0:T(8,128)}, u32[]{:S(2)}) copy-start(f32[8,16,8,128]{3,2,1,0:T(8,128)} %param.4) | copy-start | bytes 1572868
  7.2 371.0 %all-reduce.3.cloned.1.call-start = ((), (), s32[]{:S(2)}) async-start(), calls=%async_computation | async-start | bytes 262144
  8.6 14.5 %collective-permute-start = (f32[8,16,2,128]{3,2,1,0:T(2,128)S(1)}, f32[8,16,2,128]{3,2,1,0:T(2,128)S(1)}, u32[]{:S(2)}, u32[]{:S(2)}) collective-permute-start(f32[8,16,2,128]{3,2,1,0:T(2,128)S(1)} %get-tuple-element.178), channel_id=1, source_target_pairs={{0,2},{2,4},{4,6},{6,8},{8,10},{10,12},{12,14},{14,16},{16,18},{18... | collective-permute-start | bytes 393224 | tf_op jit(solution)/shard_map/ppermute | solution.py:21
  11.1 12.0 %collective-permute-start.1 = (f32[8,16,2,128]{3,2,1,0:T(2,128)S(1)}, f32[8,16,2,128]{3,2,1,0:T(2,128)S(1)}, u32[]{:S(2)}, u32[]{:S(2)}) collective-permute-start(f32[8,16,2,128]{3,2,1,0:T(2,128)S(1)} %get-tuple-element.179), channel_id=1, source_target_pairs={{2,0},{4,2},{6,4},{8,6},{10,8},{12,10},{14,12},{16,14},{18,16},{20... | collective-permute-start | bytes 393224 | tf_op jit(solution)/shard_map/ppermute | solution.py:24
  23.1 3.8 copy-start.68
  24.1 2.1 collective-permute-start.2
  25.2 1.3 collective-permute-start.3
  36.1 2.6 copy-start.18
  39.1 2.3 copy-start.14
  39.1 2.3 copy-start.13
  42.5 4.1 copy-start.9
  42.5 4.1 copy-start.11
  42.6 4.1 copy-start.27
  140.9 2.6 copy-start.59
  140.9 3.2 copy-start.21
  140.9 3.2 copy-start.34
  140.9 3.2 copy-start.50
  141.0 3.2 copy-start.52
  141.1 3.1 copy-start.10
  141.1 3.1 copy-start.12
  141.1 3.1 copy-start.20
  141.1 3.1 copy-start.33
  149.0 235.9 %copy-start.58 = (f32[17,8,128]{2,1,0:T(8,128)S(1)}, f32[17,8,128]{2,1,0:T(8,128)}, u32[]{:S(2)}) copy-start(f32[17,8,128]{2,1,0:T(8,128)} %get-tuple-element.83) | copy-start | bytes 208900
  379.1 7.2 %collective-permute-start.9 = (f32[1,128]{1,0:T(1,128)S(1)}, f32[1,128]{1,0:T(1,128)S(1)}, u32[]{:S(2)}, u32[]{:S(2)}) collective-permute-start(f32[1,128]{1,0:T(1,128)S(1)} %fusion.181), channel_id=1, source_target_pairs={{2,0},{4,2},{6,4},{8,6},{10,8},{12,10},{14,12},{16,14},{18,16},{20... | collective-permute-start | bytes 1544 | tf_op jit(solution)/shard_map/ppermute | solution.py:24
  380.5 5.9 collective-permute-start.8
  384.9 7.8 %copy-start.76 = (f32[4,1,128]{2,1,0:T(1,128)S(1)}, f32[4,1,128]{2,1,0:T(1,128)}, u32[]{:S(2)}) copy-start(f32[4,1,128]{2,1,0:T(1,128)} %param.6) | copy-start | bytes 6148
  384.9 13.8 %copy-start.19 = (f32[8,16,8,129]{3,2,1,0:T(8,128)S(1)}, f32[8,16,8,129]{3,2,1,0:T(8,128)}, u32[]{:S(2)}) copy-start(f32[8,16,8,129]{3,2,1,0:T(8,128)} %fusion.14) | copy-start | bytes 1585156
  386.4 5.5 collective-permute-start.10
  387.7 5.0 collective-permute-start.11
  392.9 92.2 %copy-start.67 = (s32[16384]{0:T(1024)S(1)}, s32[16384]{0:T(1024)}, u32[]{:S(2)}) copy-start(s32[16384]{0:T(1024)} %get-tuple-element.66) | copy-start | bytes 196612
  392.9 6.1 collective-permute-start.13
  394.3 5.1 collective-permute-start.12
  399.5 4.4 collective-permute-start.14
  400.8 3.9 collective-permute-start.15
  404.9 12.9 %collective-permute-start.17 = (f32[1,128]{1,0:T(1,128)S(1)}, f32[1,128]{1,0:T(1,128)S(1)}, u32[]{:S(2)}, u32[]{:S(2)}) collective-permute-start(f32[1,128]{1,0:T(1,128)S(1)} %fusion.177), channel_id=1, source_target_pairs={{2,0},{4,2},{6,4},{8,6},{10,8},{12,10},{14,12},{16,14},{18,16},{20... | collective-permute-start | bytes 1544 | tf_op jit(solution)/shard_map/ppermute | solution.py:24
  406.2 11.6 %collective-permute-start.16 = (f32[1,128]{1,0:T(1,128)S(1)}, f32[1,128]{1,0:T(1,128)S(1)}, u32[]{:S(2)}, u32[]{:S(2)}) collective-permute-start(f32[1,128]{1,0:T(1,128)S(1)} %fusion.177), channel_id=1, source_target_pairs={{0,2},{2,4},{4,6},{6,8},{8,10},{10,12},{12,14},{14,16},{16,18},{18... | collective-permute-start | bytes 1544 | tf_op jit(solution)/shard_map/ppermute | solution.py:21
  410.9 234.8 %collective-permute-start.4 = (f32[8,16,2,128]{3,2,1,0:T(2,128)S(1)}, f32[8,16,2,128]{3,2,1,0:T(2,128)S(1)}, u32[]{:S(2)}, u32[]{:S(2)}) collective-permute-start(f32[8,16,2,128]{3,2,1,0:T(2,128)S(1)} %get-tuple-element.176), channel_id=1, source_target_pairs={{0,2},{2,4},{4,6},{6,8},{8,10},{10,12},{12,14},{14,16},{16,18},{18... | collective-permute-start | bytes 393224 | tf_op jit(solution)/shard_map/ppermute | solution.py:21
  412.7 233.0 %collective-permute-start.5 = (f32[8,16,2,128]{3,2,1,0:T(2,128)S(1)}, f32[8,16,2,128]{3,2,1,0:T(2,128)S(1)}, u32[]{:S(2)}, u32[]{:S(2)}) collective-permute-start(f32[8,16,2,128]{3,2,1,0:T(2,128)S(1)} %get-tuple-element.177), channel_id=1, source_target_pairs={{2,0},{4,2},{6,4},{8,6},{10,8},{12,10},{14,12},{16,14},{18,16},{20... | collective-permute-start | bytes 393224 | tf_op jit(solution)/shard_map/ppermute | solution.py:24
  417.9 4.4 collective-permute-start.18
  419.2 3.9 collective-permute-start.19
  423.4 222.4 %copy-start.75 = (f32[1,128]{1,0:T(1,128)}, f32[1,128]{1,0:T(1,128)S(1)}, u32[]{:S(2)}) copy-start(f32[1,128]{1,0:T(1,128)S(1)} %fusion.175) | copy-start | bytes 1540
  645.8 1.4 collective-permute-start.6
  646.0 1.5 collective-permute-start.7
  654.5 4.1 copy-start.5
  654.6 4.1 copy-start.7
  654.6 4.1 copy-start.29
  654.6 4.1 copy-start.31
  (50 other events, 63.4 us)
Sparse Core Ops, SparseCore 0:
  136.1 241.9 all-reduce.2
where the time goes:
time: 685 us; the launch traced here: 684 us
  waiting for transfers between devices  233 us (34%)
  local copies, waits for them, and re-layouts  191 us (28%)
  other arithmetic  131 us (19%)
  blocking collectives  61.8 us (9%)
  starting transfers between devices  51.8 us (8%)
  between operations  15.3 us (2%)
    unnamed x2, waiting for transfers between devices  228 us
    gather x1, local copies, waits for them, and re-layouts, body(): footpoint_potential = whole_table[node_slot]  161 us
    scatter-add x1, other arithmetic, body(): jax.ops.segment_sum(cell_current, node_slot.reshape(-1), num_segments=NLA...  86.9 us
    all_gather x1, blocking collectives, body(): lax.all_gather(potential.reshape(-1), ('shell', 'radial'), axis=0, tiled=...  61.8 us
    ppermute x10, starting transfers between devices, padded_2(): lax.ppermute(lax.slice_in_dim(block, 0, width, axis=dim), axis, backward)  28.9 us
    ppermute x10, starting transfers between devices, padded_2(): lax.ppermute(lax.slice_in_dim(block, block.shape[dim] - width, None, axis...  22.8 us
  transfers between devices with their start and end apart: 21, of which 9 were waited for; matrix products, arithmetic and copies ran while one was open for 26% of the time, Pallas kernels for 0%

commit v1 on v0

--- a/solution.py
+++ b/solution.py
@@ -169,7 +169,15 @@
         coupled = coupled + conductance[2] * padded_panel[1:-1, :-2]
         coupled = coupled + conductance[3] * padded_panel[1:-1, 2:]
         potential = apply_blocks(coupled)
-    whole_table = lax.all_gather(potential.reshape(-1), ("shell", "radial"), axis=0, tiled=True)
+    whole_table = jnp.concatenate(
+        lax.all_to_all(
+            jnp.stack([potential.reshape(-1)] * lax.axis_size(("shell", "radial"))),
+            ("shell", "radial"),
+            0,
+            0,
+        ),
+        axis=0,
+    )
     footpoint_potential = whole_table[node_slot]
     return (state_next, potential, footpoint_potential)
 

time: 685 us -> 639 us (0.933)
  blocking collectives: 61.8 us -> 0 us
  starting transfers between devices: 51.8 us -> 67.3 us
    all_gather x1 -> x0, blocking collectives: 61.8 us -> none  [body(): lax.all_gather(potential.reshape(-1), ('shell', 'radial'), axis=0, tiled=...]
    all_to_all x0 -> x1, starting transfers between devices: none -> 13.6 us  [body(): lax.all_to_all(jnp.stack([potential.reshape(-1)] * lax.axis_size(('shell'...]
  transfers between devices with their start and end apart: 21 -> 22, of which waited for: 9 -> 9; matrix products, arithmetic and copies ran while one was open for 26% -> 7% of each run, Pallas kernels for 0% -> 0%
where the time goes in v1:
time: 639 us; the launch traced here: 638 us
  waiting for transfers between devices  233 us (36%)
  local copies, waits for them, and re-layouts  191 us (30%)
  other arithmetic  130 us (20%)
  starting transfers between devices  67.3 us (11%)
  between operations  15.4 us (2%)
    unnamed x2, waiting for transfers between devices  228 us
    gather x1, local copies, waits for them, and re-layouts, body(): footpoint_potential = whole_table[node_slot]  161 us
    scatter-add x1, other arithmetic, body(): jax.ops.segment_sum(cell_current, node_slot.reshape(-1), num_segments=NLA...  86.9 us
    ppermute x10, starting transfers between devices, padded_2(): lax.ppermute(lax.slice_in_dim(block, 0, width, axis=dim), axis, backward)  28.8 us
    ppermute x10, starting transfers between devices, padded_2(): lax.ppermute(lax.slice_in_dim(block, block.shape[dim] - width, None, axis...  24.9 us
    slice x6, local copies, waits for them, and re-layouts, pad_latitude(): return jnp.pad(field, ((0, 0), (0, 0), (0, 0), (2, 2)), mode='edge')  13.6 us
    all_to_all x1, starting transfers between devices, body(): lax.all_to_all(jnp.stack([potential.reshape(-1)] * lax.axis_size(('shell'...  13.6 us
  transfers between devices with their start and end apart: 22, of which 9 were waited for; matrix products, arithmetic and copies ran while one was open for 7% of the time, Pallas kernels for 0%

profile of v1, /device:TPU:1, one launch (start us, length us, event | category | flops | bytes accessed | tf_op | source)
XLA Modules:
  0.0 637.9 jit_solution(11354747382657837081)
XLA Ops:
  7.2 1.4 fusion.271
  8.6 2.5 collective-permute-start
  11.1 8.7 %collective-permute-start.1 = (f32[8,16,2,128]{3,2,1,0:T(2,128)S(1)}, f32[8,16,2,128]{3,2,1,0:T(2,128)S(1)}, u32[]{:S(2)}, u32[]{:S(2)}) collective-permute-start(f32[8,16,2,128]{3,2,1,0:T(2,128)S(1)} %get-tuple-element.179), channel_id=1, source_target_pairs={{2,0},{4,2},{6,4},{8,6},{10,8},{12,10},{14,12},{16,14},{18,16},{20... | collective-permute-start | bytes 393224 | tf_op jit(solution)/shard_map/ppermute | solution.py:24
  20.9 1.6 fusion.158
  23.0 0.9 pad_maximum_fusion.19
  24.0 1.2 collective-permute-start.2
  26.9 0.9 slice_subtract_fusion.4
  27.8 1.1 slice_subtract_fusion.2
  28.9 1.6 fusion.269
  30.5 2.5 copy.843
  33.0 1.2 copy.844
  36.1 2.6 pad_maximum_fusion
  39.9 1.5 multiply_reduce_fusion.31
  42.6 1.8 multiply_reduce_fusion.22
  45.1 1.6 multiply_reduce_fusion.19
  49.2 86.9 %scatter_custom_fusion = f32[32768]{0:T(1024)} fusion(s32[16384]{0:T(1024)} %bitcast.616, f32[16384]{0:T(1024)} %bitcast.617, f32[]{:T(128)} %constant.97.clone.1), kind=kCustom, calls=%fused_computation.431 | custom fusion | flops 16384 | bytes 131584 | tf_op jit(solution)/shard_map/scatter-add | solution.py:153
  136.1 2.6 slice_subtract_fusion.1
  147.7 1.3 fusion.14
  149.0 0.9 multiply_add_fusion.10
  149.9 228.2 %all-reduce.3.cloned.1.call-done = f32[32768]{0:T(1024)} async-done(((f32[32768]{0:T(1024)}), f32[32768]{0:T(1024)}) %all-reduce.3.cloned.1.call-update) | async-done | bytes 131088
  379.1 1.3 collective-permute-start.9
  380.4 4.4 collective-permute-start.8
  384.9 1.4 fusion.24
  386.4 1.3 collective-permute-start.10
  387.7 4.2 collective-permute-start.11
  392.9 1.3 collective-permute-start.13
  394.2 4.3 collective-permute-start.12
  399.3 1.3 collective-permute-start.14
  400.6 3.1 collective-permute-start.15
  404.8 1.3 collective-permute-start.17
  406.1 4.5 collective-permute-start.16
  410.7 1.8 collective-permute-start.4
  412.6 5.2 collective-permute-start.5
  417.8 1.3 collective-permute-start.18
  419.1 3.1 collective-permute-start.19
  424.0 13.6 %all-to-all-start = ((f32[256,1,128]{2,1,0:T(1,128)}), f32[256,1,128]{2,1,0:T(1,128)S(1)}, u32[]{:S(2)}, u32[]{:S(2)}) async-start(f32[256,1,128]{2,1,0:T(1,128)} %stack.3), calls=%async_computation | async-start | bytes 262144 | tf_op jit(solution)/shard_map/all_to_all | solution.py:173
  437.6 2.2 collective-permute-start.6
  441.8 1.9 fusion.268
  444.2 1.6 multiply_reduce_fusion.28
  445.8 1.4 multiply_reduce_fusion.25
  448.4 1.0 multiply_reduce_fusion.10
  450.1 1.6 multiply_reduce_fusion.7
  452.4 3.2 copy.860
  455.5 3.2 copy.861
  458.7 1.3 reshape.273
  460.4 1.0 fusion.4
  469.3 1.1 fusion.32
  470.4 160.6 %gather_fusion = f32[16384]{0:T(1024)} fusion(f32[32768]{0:T(1024)S(1)} %bitcast.596, s32[16384]{0:T(1024)S(1)} %copy-done.68), kind=kCustom, calls=%fused_computation | custom fusion | bytes 196608 | tf_op jit(solution)/shard_map/gather | solution.py:181
  (280 shorter events, 37.8 us)
Async XLA Ops:
  7.2 371.8 %copy-start = (f32[1,1,128,128]{3,2,1,0:T(8,128)S(1)}, f32[1,1,128,128]{3,2,1,0:T(8,128)}, u32[]{:S(2)}) copy-start(f32[1,1,128,128]{3,2,1,0:T(8,128)} %param.7) | copy-start | bytes 196612
  7.2 18.3 %copy-start.4 = (f32[8,16,8,128]{3,2,1,0:T(8,128)S(1)}, f32[8,16,8,128]{3,2,1,0:T(8,128)}, u32[]{:S(2)}) copy-start(f32[8,16,8,128]{3,2,1,0:T(8,128)} %param.4) | copy-start | bytes 1572868
  7.2 371.0 %all-reduce.3.cloned.1.call-start = ((), (), s32[]{:S(2)}) async-start(), calls=%async_computation.1 | async-start | bytes 262144
  8.6 14.4 %collective-permute-start = (f32[8,16,2,128]{3,2,1,0:T(2,128)S(1)}, f32[8,16,2,128]{3,2,1,0:T(2,128)S(1)}, u32[]{:S(2)}, u32[]{:S(2)}) collective-permute-start(f32[8,16,2,128]{3,2,1,0:T(2,128)S(1)} %get-tuple-element.178), channel_id=1, source_target_pairs={{0,2},{2,4},{4,6},{6,8},{8,10},{10,12},{12,14},{14,16},{16,18},{18... | collective-permute-start | bytes 393224 | tf_op jit(solution)/shard_map/ppermute | solution.py:21
  11.1 11.9 %collective-permute-start.1 = (f32[8,16,2,128]{3,2,1,0:T(2,128)S(1)}, f32[8,16,2,128]{3,2,1,0:T(2,128)S(1)}, u32[]{:S(2)}, u32[]{:S(2)}) collective-permute-start(f32[8,16,2,128]{3,2,1,0:T(2,128)S(1)} %get-tuple-element.179), channel_id=1, source_target_pairs={{2,0},{4,2},{6,4},{8,6},{10,8},{12,10},{14,12},{16,14},{18,16},{20... | collective-permute-start | bytes 393224 | tf_op jit(solution)/shard_map/ppermute | solution.py:24
  23.0 3.9 copy-start.69
  24.0 2.2 collective-permute-start.2
  25.2 1.3 collective-permute-start.3
  42.5 4.2 copy-start.9
  42.5 4.1 copy-start.11
  42.6 4.1 copy-start.28
  141.0 3.2 copy-start.23
  141.0 3.2 copy-start.35
  141.0 3.2 copy-start.51
  141.0 3.2 copy-start.53
  141.2 3.1 copy-start.10
  141.2 3.1 copy-start.12
  141.2 3.1 copy-start.22
  141.2 3.1 copy-start.34
  149.0 235.9 %copy-start.59 = (f32[17,8,128]{2,1,0:T(8,128)S(1)}, f32[17,8,128]{2,1,0:T(8,128)}, u32[]{:S(2)}) copy-start(f32[17,8,128]{2,1,0:T(8,128)} %get-tuple-element.83) | copy-start | bytes 208900
  379.1 7.2 %collective-permute-start.9 = (f32[1,128]{1,0:T(1,128)S(1)}, f32[1,128]{1,0:T(1,128)S(1)}, u32[]{:S(2)}, u32[]{:S(2)}) collective-permute-start(f32[1,128]{1,0:T(1,128)S(1)} %fusion.181), channel_id=1, source_target_pairs={{2,0},{4,2},{6,4},{8,6},{10,8},{12,10},{14,12},{16,14},{18,16},{20... | collective-permute-start | bytes 1544 | tf_op jit(solution)/shard_map/ppermute | solution.py:24
  380.4 5.9 collective-permute-start.8
  384.9 7.8 %copy-start.77 = (f32[4,1,128]{2,1,0:T(1,128)S(1)}, f32[4,1,128]{2,1,0:T(1,128)}, u32[]{:S(2)}) copy-start(f32[4,1,128]{2,1,0:T(1,128)} %param.6) | copy-start | bytes 6148
  384.9 13.7 %copy-start.21 = (f32[8,16,8,129]{3,2,1,0:T(8,128)S(1)}, f32[8,16,8,129]{3,2,1,0:T(8,128)}, u32[]{:S(2)}) copy-start(f32[8,16,8,129]{3,2,1,0:T(8,128)} %fusion.14) | copy-start | bytes 1585156
  386.4 5.5 collective-permute-start.10
  387.7 5.0 collective-permute-start.11
  392.9 6.0 collective-permute-start.13
  394.2 5.1 collective-permute-start.12
  399.3 4.4 collective-permute-start.14
  400.6 3.9 collective-permute-start.15
  404.8 13.0 %collective-permute-start.17 = (f32[1,128]{1,0:T(1,128)S(1)}, f32[1,128]{1,0:T(1,128)S(1)}, u32[]{:S(2)}, u32[]{:S(2)}) collective-permute-start(f32[1,128]{1,0:T(1,128)S(1)} %fusion.177), channel_id=1, source_target_pairs={{2,0},{4,2},{6,4},{8,6},{10,8},{12,10},{14,12},{16,14},{18,16},{20... | collective-permute-start | bytes 1544 | tf_op jit(solution)/shard_map/ppermute | solution.py:24
  406.1 11.6 %collective-permute-start.16 = (f32[1,128]{1,0:T(1,128)S(1)}, f32[1,128]{1,0:T(1,128)S(1)}, u32[]{:S(2)}, u32[]{:S(2)}) collective-permute-start(f32[1,128]{1,0:T(1,128)S(1)} %fusion.177), channel_id=1, source_target_pairs={{0,2},{2,4},{4,6},{6,8},{8,10},{10,12},{12,14},{14,16},{16,18},{18... | collective-permute-start | bytes 1544 | tf_op jit(solution)/shard_map/ppermute | solution.py:21
  410.7 30.5 %copy-start.70 = (pred[20]{0:T(512)(128)(4,1)S(1)}, pred[20]{0:T(512)(128)(4,1)}, u32[]{:S(2)}) copy-start(pred[20]{0:T(512)(128)(4,1)} %copy-done.69) | copy-start | bytes 64
  410.7 26.8 %collective-permute-start.4 = (f32[8,16,2,128]{3,2,1,0:T(2,128)S(1)}, f32[8,16,2,128]{3,2,1,0:T(2,128)S(1)}, u32[]{:S(2)}, u32[]{:S(2)}) collective-permute-start(f32[8,16,2,128]{3,2,1,0:T(2,128)S(1)} %get-tuple-element.176), channel_id=1, source_target_pairs={{0,2},{2,4},{4,6},{6,8},{8,10},{10,12},{12,14},{14,16},{16,18},{18... | collective-permute-start | bytes 393224 | tf_op jit(solution)/shard_map/ppermute | solution.py:21
  412.6 25.0 %collective-permute-start.5 = (f32[8,16,2,128]{3,2,1,0:T(2,128)S(1)}, f32[8,16,2,128]{3,2,1,0:T(2,128)S(1)}, u32[]{:S(2)}, u32[]{:S(2)}) collective-permute-start(f32[8,16,2,128]{3,2,1,0:T(2,128)S(1)} %get-tuple-element.177), channel_id=1, source_target_pairs={{2,0},{4,2},{6,4},{8,6},{10,8},{12,10},{14,12},{16,14},{18,16},{20... | collective-permute-start | bytes 393224 | tf_op jit(solution)/shard_map/ppermute | solution.py:24
  417.8 4.4 collective-permute-start.18
  419.1 3.9 collective-permute-start.19
  423.2 18.4 %copy-start.76 = (f32[1,128]{1,0:T(1,128)}, f32[1,128]{1,0:T(1,128)S(1)}, u32[]{:S(2)}) copy-start(f32[1,128]{1,0:T(1,128)S(1)} %fusion.175) | copy-start | bytes 1540
  424.0 46.4 %all-to-all-start = ((f32[256,1,128]{2,1,0:T(1,128)}), f32[256,1,128]{2,1,0:T(1,128)S(1)}, u32[]{:S(2)}, u32[]{:S(2)}) async-start(f32[256,1,128]{2,1,0:T(1,128)} %stack.3), calls=%async_computation | async-start | bytes 262144 | tf_op jit(solution)/shard_map/all_to_all | solution.py:173
  437.6 3.2 collective-permute-start.6
  439.9 1.3 collective-permute-start.7
  444.1 3.1 copy-start.18
  444.2 3.1 copy-start.46
  448.4 3.4 copy-start.5
  448.4 3.4 copy-start.7
  448.4 3.3 copy-start.30
  448.4 3.3 copy-start.32
  470.4 160.6 %copy-start.1 = (f32[1,1,128,128]{3,2,1,0:T(8,128)S(1)}, f32[1,1,128,128]{3,2,1,0:T(8,128)}, u32[]{:S(2)}) copy-start(f32[1,1,128,128]{3,2,1,0:T(8,128)} %param.7) | copy-start | bytes 196612
  (52 other events, 71.4 us)
Sparse Core Ops, SparseCore 0:
  136.2 241.9 all-reduce.2
